TPU v7x, 256 devices: a whole 4x4x8 slice. The times are simulated.
256 devices in a mesh: seg: 4 (over x), ctx: 64 (over y, z, core).
Axes of the slice: x: 4, y: 4, z: 8, core: 2. Of those that a mesh axis runs over, the one named last changes fastest.
Arguments:
- hidden_in: bfloat16 [32768, 1024], P(('seg', 'ctx')), may hold values from -6 to 6
- queries: bfloat16 [32768, 1024], P(('seg', 'ctx')), may hold values from -6 to 6
- key_rows: bfloat16 [32768, 1024], P(('seg', 'ctx')), may hold values from -6 to 6
- values: bfloat16 [32768, 1024], P(('seg', 'ctx')), may hold values from -6 to 6
- norm_gain: float32 [1024], replicated, may hold values from 0.5 to 1.5
- out_proj: bfloat16 [1024, 1024], replicated, may hold values from -0.1875 to 0.1875
- moe_gain: float32 [1024], replicated, may hold values from 0.5 to 1.5
- w_gate: bfloat16 [64, 1024, 896], P('ctx'), may hold values from -0.1875 to 0.1875
- w_up: bfloat16 [64, 1024, 896], P('ctx'), may hold values from -0.1875 to 0.1875
- w_down: bfloat16 [64, 896, 1024], P('ctx'), may hold values from -0.1875 to 0.1875
- expert_ids: int32 [32768, 8], P(('seg', 'ctx')), may hold values from 0 to 63, all different within a row; in each aligned block of 128 rows (0 to 127, 128 to 255, ...) at most 24 rows name the same one
- route_scale: int32 [32768, 8], P(('seg', 'ctx')), may hold values from 1 to 4095
Outputs:
- layer_out: bfloat16 [32768, 1024], P(('seg', 'ctx'))
Inputs may be any that keep to these rules, and one draw needn't show every extreme that they name: `expert_ids`: each row names 8 different experts. Among the rows of one device no expert is named more than 24 times, and in every draw some device names some expert exactly 24 times.
All inputs are finite; a program needn't handle non-finite values.
Results may differ from a plain program's by a relative error of at most 0.0075.
Values may be sent and summed in bfloat16 or wider, within the bound.
A program may use at most 192 MiB of HBM per device.

v0:
```python
import jax
import jax.numpy as jnp
from jax import lax
from jax.sharding import Mesh
from jax.sharding import PartitionSpec as P

HEADS = 8
HEAD = 128
D = 1024
TOP = 8
SEG_CTX = ("seg", "ctx_0", "ctx_1", "ctx_2")
CTX = ("ctx_0", "ctx_1", "ctx_2")


def filled_with(shard, identity):
    return jnp.broadcast_to(jnp.asarray(identity, shard.dtype), shard.shape)


def entering(shard, axes, combine, identity):
    before = start = filled_with(shard, identity)
    so_far = shard
    for axis in reversed(axes):
        peers, index = (lax.axis_size(axis), lax.axis_index(axis))
        pieces = lax.all_gather(so_far, axis)
        inside, so_far = (start, start)
        for k in range(peers):
            passed = k < index
            so_far = combine(so_far, pieces[k])
            inside = jnp.where(passed, so_far, inside)
        before = combine(inside, before)
    return before


def rms_scale(rows, gain):
    mean_sq = jnp.mean(rows * rows, axis=1, keepdims=True)
    return rows * lax.rsqrt(mean_sq + 1e-06) * gain[None, :]


def add_states(earlier, later):
    return earlier + later


def expert_rows(arrived, w_gate, w_up, w_down):
    sources, slots = (arrived.shape[0], arrived.shape[1])
    rows = arrived.reshape(sources * slots, D)
    gate = jnp.dot(rows, w_gate[0], preferred_element_type=jnp.float32)
    upper = jnp.dot(rows, w_up[0], preferred_element_type=jnp.float32)
    inner = (jax.nn.silu(gate) * upper).astype(jnp.bfloat16)
    result = jnp.dot(inner, w_down[0], preferred_element_type=jnp.float32).astype(jnp.bfloat16)
    return result.reshape(sources, slots, D)


def body(
    hidden_in,
    queries,
    key_rows,
    values,
    norm_gain,
    out_proj,
    moe_gain,
    w_gate,
    w_up,
    w_down,
    expert_ids,
    route_scale,
):
    ntok = queries.shape[0]
    high = lax.Precision.HIGHEST
    q_loc = queries.astype(jnp.float32).reshape(ntok, HEADS, HEAD)
    k_loc = key_rows.astype(jnp.float32).reshape(ntok, HEADS, HEAD)
    v_loc = values.astype(jnp.float32).reshape(ntok, HEADS, HEAD)
    own_state = jnp.einsum("thd,the->hde", k_loc, v_loc, precision=high)
    empty = jnp.zeros_like(own_state)
    earlier = entering(own_state, SEG_CTX, add_states, empty)
    causal = jnp.arange(ntok)[:, None] >= jnp.arange(ntok)[None, :]
    scores = jnp.einsum("thd,shd->hts", q_loc, k_loc, precision=high)
    scores = jnp.where(causal[None, :, :], scores, jnp.zeros((), jnp.float32))
    inside = jnp.einsum("hts,she->the", scores, v_loc, precision=high)
    carried = jnp.einsum("thd,hde->the", q_loc, earlier, precision=high)
    attended = (carried + inside).reshape(ntok, D)
    normed = rms_scale(attended, norm_gain).astype(jnp.bfloat16)
    mixed = hidden_in.astype(jnp.float32) + jnp.dot(
        normed, out_proj, preferred_element_type=jnp.float32
    )
    routed = rms_scale(mixed, moe_gain).astype(jnp.bfloat16)
    experts_all = lax.axis_size(CTX) * w_gate.shape[0]
    capacity = min(ntok, 3 * ntok * TOP // (2 * experts_all))
    expert_grid = jnp.arange(experts_all, dtype=jnp.int32)
    chosen = (expert_ids[:, :, None] == expert_grid[None, None, :]).astype(jnp.float32)
    per_token = jnp.sum(chosen, axis=1)
    lower = (jnp.arange(ntok)[:, None] > jnp.arange(ntok)[None, :]).astype(jnp.float32)
    before_tok = jnp.dot(lower, per_token, precision=high)
    position = jnp.sum(chosen * before_tok[:, None, :], axis=2).astype(jnp.int32)
    slot_id = expert_ids * capacity + position
    slot_grid = jnp.arange(experts_all * capacity, dtype=jnp.int32)
    placing = jnp.sum(
        (slot_id[:, :, None] == slot_grid[None, None, :]).astype(jnp.float32), axis=1
    ).astype(jnp.bfloat16)
    outgoing = jnp.einsum("ts,td->sd", placing, routed, preferred_element_type=jnp.float32)
    outgoing = outgoing.astype(jnp.bfloat16).reshape(experts_all, capacity, D)
    came_back = lax.all_to_all(
        expert_rows(
            lax.all_to_all(outgoing, CTX, split_axis=0, concat_axis=0, tiled=True),
            w_gate,
            w_up,
            w_down,
        ),
        CTX,
        split_axis=0,
        concat_axis=0,
        tiled=True,
    )
    back_rows = came_back.reshape(experts_all * capacity, D)
    picked = back_rows[slot_id.reshape(-1)].reshape(ntok, TOP, D).astype(jnp.float32)
    scales = route_scale.astype(jnp.float32)
    weight = scales / jnp.sum(scales, axis=1, keepdims=True)
    combined = jnp.sum(weight[:, :, None] * picked, axis=1)
    return (mixed + combined).astype(jnp.bfloat16)


def solution(mesh):
    finer = Mesh(
        mesh.devices.reshape(mesh.shape["seg"], 4, 8, 2), ("seg", "ctx_0", "ctx_1", "ctx_2")
    )
    placed = (
        P(SEG_CTX, None),
        P(SEG_CTX, None),
        P(SEG_CTX, None),
        P(SEG_CTX, None),
        P(),
        P(),
        P(),
        P(CTX, None, None),
        P(CTX, None, None),
        P(CTX, None, None),
        P(SEG_CTX, None),
        P(SEG_CTX, None),
    )
    return jax.shard_map(
        body, mesh=finer, in_specs=placed, out_specs=P(SEG_CTX, None), check_vma=False
    )
```

profile of v0, /device:TPU:1, one launch (start us, length us, event | category | flops | bytes accessed | tf_op | source)
XLA Modules:
  0.0 365.7 jit_solution(16872688503069752293)
XLA Ops:
  6.5 0.0 copy-start
  6.5 0.0 all-gather.11.cloned.1.call-start
  6.5 1.3 copy.55
  7.8 2.1 fusion.42
  9.9 0.0 all-gather.11.cloned.1.call-update
  9.9 0.0 all-gather.13.cloned.1.call-start
  10.0 19.0 %all-gather.11.cloned.1.call-done = f32[16,128,128]{2,1,0:T(8,128)} async-done(((f32[8,128,128]{2,1,0:T(8,128)}), f32[16,128,128]{2,1,0:T(8,128)}) %all-gather.11.cloned.1.call-update) | async-done | bytes 1048592 | tf_op jit(solution)/shard_map/all_gather | solution.py:24
  28.9 2.1 slice_add_fusion.11
  31.0 0.0 all-gather.13.cloned.1.call-update
  31.0 0.0 all-gather.7.cloned.1.call-start
  31.1 55.3 %all-gather.13.cloned.1.call-done = f32[64,128,128]{2,1,0:T(8,128)} async-done(((f32[8,128,128]{2,1,0:T(8,128)}), f32[64,128,128]{2,1,0:T(8,128)}) %all-gather.13.cloned.1.call-update) | async-done | bytes 4194320 | tf_op jit(solution)/shard_map/all_gather | solution.py:24
  86.3 3.4 fusion.11
  89.8 0.0 all-gather.7.cloned.1.call-update
  89.8 0.0 copy-start.2
  89.8 0.0 copy-start.3
  89.8 0.0 all-gather.9.cloned.1.call-start
  89.8 32.0 %all-gather.7.cloned.1.call-done = f32[4,8,128,128]{3,2,1,0:T(8,128)} async-done(((f32[1,8,128,128]{3,2,1,0:T(8,128)}), f32[4,8,128,128]{3,2,1,0:T(8,128)}) %all-gather.7.cloned.1.call-update) | async-done | bytes 2097168 | tf_op jit(solution)/shard_map/all_gather | solution.py:24
  121.9 2.4 slice_add_fusion.3
  124.3 0.0 all-gather.9.cloned.1.call-update
  124.3 0.0 copy-done.6
  124.4 0.2 fusion.72
  124.7 0.1 copy.52
  124.8 3.9 %convert_reduce_fusion = bf16[128,1536]{1,0:T(8,128)(2,1)} fusion(s32[128,8]{1,0:T(8,128)S(1)} %copy.52), kind=kLoop, calls=%fused_computation.1 | loop fusion | flops 4521984 | bytes 397312 | tf_op jit(solution)/shard_map/reduce_sum | solution.py:96
  128.7 1.3 convolution_select_fusion
  130.0 1.5 convolution_bitcast_fusion
  131.5 26.3 %all-gather.9.cloned.1.call-done = f32[4,8,128,128]{3,2,1,0:T(8,128)} async-done(((f32[1,8,128,128]{3,2,1,0:T(8,128)}), f32[4,8,128,128]{3,2,1,0:T(8,128)}) %all-gather.9.cloned.1.call-update) | async-done | bytes 2097168 | tf_op jit(solution)/shard_map/all_gather | solution.py:24
  157.8 0.0 copy-done.2
  157.8 0.0 copy-done.3
  157.8 4.8 %multiply_reduce_fusion.1 = (f32[128]{0:T(128)S(1)}, f32[128,8,128]{0,2,1:T(8,128)S(1)}) fusion(f32[128,8,128]{0,2,1:T(8,128)} %convolution_bitcast_fusion, f32[4,8,128,128]{3,2,1,0:T(8,128)} %all-gather.9.cloned.1.call-done, f32[1,8,128,128]{3,2,1,0:T(8,128)S(1)} %copy-done.3, f32[8,128,128]{2,1,0:T(8,128)} %get-tuple-element.6, ...), kind=kOutput, calls=%fused_computation.55 | convolution fusion | flops 205782912 | bytes 10748434 | tf_op jit(solution)/shard_map/thd,hde->the/dot_general | solution.py:79
  162.6 0.0 copy-start.4
  162.6 0.0 copy-start.9
  162.6 0.2 fusion.15
  162.9 0.6 multiply_reduce_fusion
  163.4 0.2 copy-done.4
  163.6 0.0 copy-done.9
  163.6 1.0 convolution_convert_fusion
  164.6 0.0 copy-start.10
  164.7 84.3 %all_to_all.10 = bf16[64,24,1024]{2,1,0:T(8,128)(2,1)S(1)} all-to-all(bf16[64,24,1024]{2,1,0:T(8,128)(2,1)S(1)} %bitcast.120), channel_id=1, replica_groups=mesh['seg'=4,'ctx_0'=4,'ctx_1'=8,'ctx_2'=2] {'ctx_0','ctx_1','ctx_2'}, dimensions={0} | all-to-all | bytes 6291456 | tf_op jit(solution)/shard_map/all_to_all | solution.py:103
  248.9 1.7 copy-done.1
  250.6 5.2 %fusion.4 = f32[1536,896]{1,0:T(8,128)} fusion(bf16[1536,1024]{1,0:T(8,128)(2,1)S(1)} %bitcast.122, bf16[1,1024,896]{2,1,0:T(8,128)(2,1)S(1)} %copy-done.10), kind=kOutput, calls=%fused_computation.10 | convolution fusion | flops 2818572288 | bytes 10485760 | tf_op jit(solution)/shard_map/dot_general | solution.py:46
  255.8 11.5 %convolution_convert_fusion.1 = bf16[1536,1024]{1,0:T(8,128)(2,1)} fusion(f32[1536,896]{1,0:T(8,128)} %fusion.4, bf16[1536,1024]{1,0:T(8,128)(2,1)} %bitcast.123, bf16[1,896,1024]{2,1,0:T(8,128)(2,1)} %param.21, bf16[1,1024,896]{2,1,0:T(8,128)(2,1)} %param.20), kind=kOutput, calls=%fused_computation.7 | convolution fusion | flops 5646974976 | bytes 15466496 | tf_op jit(solution)/shard_map/dot_general | solution.py:49
  267.2 6.5 %all-to-all-start.1 = ((bf16[64,24,1024]{2,1,0:T(8,128)(2,1)}), bf16[64,24,1024]{2,1,0:T(8,128)(2,1)}, u32[]{:S(2)}, u32[]{:S(2)}) async-start(bf16[64,24,1024]{2,1,0:T(8,128)(2,1)} %bitcast.121), calls=%async_computation.1 | async-start | bytes 6291456 | tf_op jit(solution)/shard_map/all_to_all | solution.py:101
  273.7 0.1 reshape.144
  273.9 0.1 copy.51
  274.0 73.1 %all-to-all-done.1 = bf16[64,24,1024]{2,1,0:T(8,128)(2,1)} async-done(((bf16[64,24,1024]{2,1,0:T(8,128)(2,1)}), bf16[64,24,1024]{2,1,0:T(8,128)(2,1)}, u32[]{:S(2)}, u32[]{:S(2)}) %all-to-all-start.1) | async-done | bytes 3145760 | tf_op jit(solution)/shard_map/all_to_all | solution.py:101
  347.2 8.3 %gather_fusion = bf16[1024,1024]{1,0:T(8,128)(2,1)} fusion(bf16[1536,1024]{1,0:T(8,128)(2,1)} %bitcast.15, s32[1024]{0:T(1024)S(1)} %broadcast_clamp_fusion), kind=kCustom, calls=%fused_computation | custom fusion | bytes 4198400 | tf_op jit(solution)/shard_map/gather | solution.py:114
  355.4 2.9 fusion
  358.4 0.8 add_convert_fusion
  (20 shorter events, 0.2 us)
Async XLA Ops:
  6.5 156.3 %copy-start = (bf16[1024,1024]{1,0:T(8,128)(2,1)S(1)}, bf16[1024,1024]{1,0:T(8,128)(2,1)}, u32[]{:S(2)}) copy-start(bf16[1024,1024]{1,0:T(8,128)(2,1)} %param.17) | copy-start | bytes 6291460
  6.5 22.4 %all-gather.11.cloned.1.call-start = ((), (), s32[]{:S(2)}) async-start(), calls=%async_computation.4 | async-start | bytes 1572864 | tf_op jit(solution)/shard_map/all_gather | solution.py:24
  9.9 76.4 %all-gather.13.cloned.1.call-start = ((), (), s32[]{:S(2)}) async-start(), calls=%async_computation.5 | async-start | bytes 4718592 | tf_op jit(solution)/shard_map/all_gather | solution.py:24
  31.0 90.9 %all-gather.7.cloned.1.call-start = ((), (), s32[]{:S(2)}) async-start(), calls=%async_computation.2 | async-start | bytes 2621440 | tf_op jit(solution)/shard_map/all_gather | solution.py:24
  89.7 34.6 %copy-start.6 = (s32[128,8]{0,1:T(8,128)S(1)}, s32[128,8]{0,1:T(8,128)}, u32[]{:S(2)}) copy-start(s32[128,8]{0,1:T(8,128)} %param.22) | copy-start | bytes 12292
  89.8 68.0 %copy-start.2 = (f32[8,128,128]{2,1,0:T(8,128)S(1)}, f32[8,128,128]{2,1,0:T(8,128)}, u32[]{:S(2)}) copy-start(f32[8,128,128]{2,1,0:T(8,128)} %slice_add_fusion.11) | copy-start | bytes 1572868
  89.8 68.0 %copy-start.3 = (f32[1,8,128,128]{3,2,1,0:T(8,128)S(1)}, f32[1,8,128,128]{3,2,1,0:T(8,128)}, u32[]{:S(2)}) copy-start(f32[1,8,128,128]{3,2,1,0:T(8,128)} %get-tuple-element.5) | copy-start | bytes 1572868
  89.8 68.0 %all-gather.9.cloned.1.call-start = ((), (), s32[]{:S(2)}) async-start(), calls=%async_computation.3 | async-start | bytes 2621440 | tf_op jit(solution)/shard_map/all_gather | solution.py:24
  157.8 4.8 %copy-start.8 = (f32[1024]{0:T(1024)S(1)}, f32[1024]{0:T(1024)}, u32[]{:S(2)}) copy-start(f32[1024]{0:T(1024)} %param.16) | copy-start | bytes 12292
  157.8 5.1 %copy-start.5 = (bf16[128,1024]{1,0:T(8,128)(2,1)S(1)}, bf16[128,1024]{1,0:T(8,128)(2,1)}, u32[]{:S(2)}) copy-start(bf16[128,1024]{1,0:T(8,128)(2,1)} %param.12) | copy-start | bytes 786436
  162.6 1.0 copy-start.4
  162.6 1.0 copy-start.9
  164.6 86.0 %copy-start.10 = (bf16[1,1024,896]{2,1,0:T(8,128)(2,1)S(1)}, bf16[1,1024,896]{2,1,0:T(8,128)(2,1)}, u32[]{:S(2)}) copy-start(bf16[1,1024,896]{2,1,0:T(8,128)(2,1)} %param.19) | copy-start | bytes 5505028
  248.9 1.7 copy-start.1
  267.2 6.6 %copy-start.7 = (s32[128,8]{0,1:T(8,128)S(1)}, s32[128,8]{0,1:T(8,128)}, u32[]{:S(2)}) copy-start(s32[128,8]{0,1:T(8,128)} %param.23) | copy-start | bytes 12292
  267.2 79.9 %all-to-all-start.1 = ((bf16[64,24,1024]{2,1,0:T(8,128)(2,1)}), bf16[64,24,1024]{2,1,0:T(8,128)(2,1)}, u32[]{:S(2)}, u32[]{:S(2)}) async-start(bf16[64,24,1024]{2,1,0:T(8,128)(2,1)} %bitcast.121), calls=%async_computation.1 | async-start | bytes 6291456 | tf_op jit(solution)/shard_map/all_to_all | solution.py:101
Sparse Core Ops, SparseCore 0:
  10.0 18.8 all-gather.10
  31.1 55.1 all-gather.12
  89.9 31.9 all-gather.6
  124.4 33.3 all-gather.8
where the time goes:
time: 366 us
  waiting for transfers between devices  206 us (56%)
  blocking collectives  84.3 us (23%)
  matrix products  28.1 us (8%)
  other arithmetic  15.8 us (4%)
  between operations  13.4 us (4%)
  local copies, waits for them, and re-layouts  11.8 us (3%)
  starting transfers between devices  6.62 us (2%)
    all_gather x4, waiting for transfers between devices, entering(): pieces = lax.all_gather(so_far, axis)  133 us
    all_to_all x1, blocking collectives, body(): lax.all_to_all(outgoing, CTX, split_axis=0, concat_axis=0, tiled=True)  84.3 us
    all_to_all x1, waiting for transfers between devices, body(): lax.all_to_all(expert_rows(lax.all_to_all(outgoing, CTX, split_axis=0, co...  73.1 us
    dot_general x1, matrix products, expert_rows(): jnp.dot(inner, w_down[0], preferred_element_type=jnp.float32)  11.5 us
    gather x1, local copies, waits for them, and re-layouts, body(): back_rows[slot_id.reshape(-1)].reshape(ntok, TOP, D).astype(jnp.float32)  8.29 us
    add x3, other arithmetic, add_states(): return earlier + later  7.86 us
  transfers between devices with their start and end apart: 5, of which 5 were waited for; matrix products, arithmetic and copies ran while one was open for 2% of the time, Pallas kernels for 0%

commit v1 on v0

--- a/solution.py
+++ b/solution.py
@@ -1,6 +1,10 @@
+import functools
+
 import jax
 import jax.numpy as jnp
 from jax import lax
+from jax.experimental import pallas as pl
+from jax.experimental.pallas import tpu as pltpu
 from jax.sharding import Mesh
 from jax.sharding import PartitionSpec as P
 
@@ -8,36 +12,193 @@
 HEAD = 128
 D = 1024
 TOP = 8
+NTOK = 128
 SEG_CTX = ("seg", "ctx_0", "ctx_1", "ctx_2")
 CTX = ("ctx_0", "ctx_1", "ctx_2")
-
-
-def filled_with(shard, identity):
-    return jnp.broadcast_to(jnp.asarray(identity, shard.dtype), shard.shape)
-
-
-def entering(shard, axes, combine, identity):
-    before = start = filled_with(shard, identity)
-    so_far = shard
-    for axis in reversed(axes):
-        peers, index = (lax.axis_size(axis), lax.axis_index(axis))
-        pieces = lax.all_gather(so_far, axis)
-        inside, so_far = (start, start)
-        for k in range(peers):
-            passed = k < index
-            so_far = combine(so_far, pieces[k])
-            inside = jnp.where(passed, so_far, inside)
-        before = combine(inside, before)
-    return before
-
-
-def rms_scale(rows, gain):
+MESH = pl.DeviceIdType.MESH
+F32 = jnp.float32
+BF16 = jnp.bfloat16
+NX, NY, NZ, NC = 4, 4, 8, 2
+PIECE = 64
+
+
+def iota(shape, axis):
+    return lax.broadcasted_iota(jnp.int32, shape, axis)
+
+
+def dot(a, b, dims=((1,), (0,))):
+    return lax.dot_general(a, b, (dims, ((), ())), preferred_element_type=F32)
+
+
+def rms(rows, gain):
     mean_sq = jnp.mean(rows * rows, axis=1, keepdims=True)
-    return rows * lax.rsqrt(mean_sq + 1e-06) * gain[None, :]
-
-
-def add_states(earlier, later):
-    return earlier + later
+    return rows * lax.rsqrt(mean_sq + 1e-06) * gain
+
+
+def place():
+    return tuple(lax.axis_index(a) for a in SEG_CTX)
+
+
+def barrier(partners):
+    sem = pltpu.get_barrier_semaphore()
+    for p in partners:
+        pl.semaphore_signal(sem, inc=1, device_id=p, device_id_type=MESH)
+    pl.semaphore_wait(sem, len(partners))
+
+
+def remote(src, dst, ssem, rsem, dev):
+    return pltpu.make_async_remote_copy(
+        src_ref=src, dst_ref=dst, send_sem=ssem, recv_sem=rsem, device_id=dev, device_id_type=MESH
+    )
+
+
+def front_kernel(
+    q, k, v, hid, ngain, wo, mgain, ids, scl,
+    mixed, routed, meta,
+    s_out, s_in, c_out, c_in, d_out, d_in, p_out, p_in, inside,
+    ss, rs, sc, rc, sd, rd, sp, rp,
+):
+    x, y, z, c = place()
+    me = z * NC + c
+    column = []
+    for dz in range(NZ):
+        for dc in range(NC):
+            if dz or dc:
+                column.append((dz * NC + dc, (lax.rem(z + dz, NZ), lax.rem(c + dc, NC))))
+    ys = [(o, lax.rem(y + o, NY)) for o in range(1, NY)]
+    xs = [(o, lax.rem(x + o, NX)) for o in range(1, NX)]
+    barrier(
+        [(x, y, zz, cc) for _, (zz, cc) in column]
+        + [(x, yy, z, c) for _, yy in ys]
+        + [(xx, y, z, c) for _, xx in xs]
+    )
+
+    rows = NZ * NC * 16
+    eye = (iota((NTOK, NTOK), 0) == iota((NTOK, NTOK), 1)).astype(F32)
+    idt = lax.dot_general(
+        ids[...].astype(F32), eye, (((0,), (0,)), ((), ())),
+        precision=lax.Precision.HIGHEST, preferred_element_type=F32,
+    )
+    sct = lax.dot_general(
+        scl[...].astype(F32), eye, (((0,), (0,)), ((), ())),
+        precision=lax.Precision.HIGHEST, preferred_element_type=F32,
+    )
+    r = iota((rows, NTOK), 0)
+    owner = (lax.rem(y + r % 4, NY) * (NZ * NC) + r // 16).astype(F32)
+    kind = (r % 16) // 4
+    chosen = jnp.zeros((rows, NTOK), F32)
+    scale = jnp.zeros((rows, NTOK), F32)
+    for j in range(TOP):
+        hit = owner == idt[j : j + 1, :]
+        chosen = jnp.where(hit, 1.0, chosen)
+        scale = jnp.where(hit, sct[j : j + 1, :], scale)
+    earlier = (iota((NTOK, NTOK), 0) < iota((NTOK, NTOK), 1)).astype(BF16)
+    pos = jnp.where(chosen > 0.5, dot(chosen.astype(BF16), earlier), -1.0)
+    weight = scale / jnp.sum(sct, axis=0, keepdims=True)
+    whi = weight.astype(BF16).astype(F32)
+    table = jnp.where(kind == 0, pos, jnp.where(kind == 1, whi, jnp.where(kind == 2, weight - whi, 0.0)))
+    s_out[:, PIECE:, :] = table.astype(BF16).reshape(NZ * NC, 16, NTOK)
+
+    for h in range(HEADS):
+        cols = slice(h * HEAD, (h + 1) * HEAD)
+        state = dot(k[:, cols], v[:, cols], ((0,), (0,)))
+        for half in range(NC):
+            s_out[h * NC + half, :PIECE, :] = state[half * PIECE : (half + 1) * PIECE, :].astype(BF16)
+    first = []
+    for o, (zz, cc) in column:
+        cp = remote(s_out.at[zz * NC + cc], s_in.at[me], ss.at[o], rs.at[o], (x, y, zz, cc))
+        cp.start()
+        first.append(cp)
+    s_in[me] = s_out[me]
+
+    causal = iota((NTOK, NTOK), 0) >= iota((NTOK, NTOK), 1)
+    for h in range(HEADS):
+        cols = slice(h * HEAD, (h + 1) * HEAD)
+        scores = jnp.where(causal, dot(q[:, cols], k[:, cols], ((1,), (1,))), 0.0)
+        hi = scores.astype(BF16)
+        lo = (scores - hi.astype(F32)).astype(BF16)
+        inside[:, cols] = dot(hi, v[:, cols]) + dot(lo, v[:, cols])
+
+    for cp in first:
+        cp.wait()
+    total = jnp.zeros((PIECE, HEAD), F32)
+    for i in range(NZ * NC):
+        total = total + s_in[i, :PIECE, :].astype(F32)
+    c_out[...] = total
+    second = []
+    for o, yy in ys:
+        cp = remote(c_out, c_in.at[o], sc.at[o], rc.at[o], (x, yy, z, c))
+        cp.start()
+        second.append(cp)
+    meta[...] = s_in[:, PIECE:, :]
+    for cp in second:
+        cp.wait()
+    before = jnp.zeros((PIECE, HEAD), F32)
+    whole = total
+    for o in range(1, NY):
+        before = before + jnp.where(y >= o, c_in[o], 0.0)
+        whole = whole + c_in[o]
+    d_out[...] = whole
+    third = []
+    for o, xx in xs:
+        cp = remote(d_out, d_in.at[o], sd.at[o], rd.at[o], (xx, y, z, c))
+        cp.start()
+        third.append(cp)
+    for cp in third:
+        cp.wait()
+    for o in range(1, NX):
+        before = before + jnp.where(x >= o, d_in[o], 0.0)
+    for i in range(NZ * NC):
+        p_out[i] = before.astype(BF16)
+        before = before + s_in[i, :PIECE, :].astype(F32)
+    fourth = []
+    for o, (zz, cc) in column:
+        cp = remote(p_out.at[zz * NC + cc], p_in.at[me], sp.at[o], rp.at[o], (x, y, zz, cc))
+        cp.start()
+        fourth.append(cp)
+    p_in[me] = p_out[me]
+    for cp in fourth:
+        cp.wait()
+
+    for h in range(HEADS):
+        cols = slice(h * HEAD, (h + 1) * HEAD)
+        state = p_in[h * NC : (h + 1) * NC].reshape(HEAD, HEAD)
+        inside[:, cols] = inside[:, cols] + dot(q[:, cols], state)
+    normed = rms(inside[...], ngain[...]).astype(BF16)
+    for n in range(0, D, 256):
+        cols = slice(n, n + 256)
+        mixed[:, cols] = hid[:, cols].astype(F32) + dot(normed, wo[:, cols])
+    routed[...] = rms(mixed[...], mgain[...]).astype(BF16)
+
+
+def front(q, k, v, hid, ngain, wo, mgain, ids, scl):
+    sem = pltpu.SemaphoreType.DMA
+    vmem = pl.BlockSpec(memory_space=pltpu.VMEM)
+    col = NZ * NC
+    return pl.pallas_call(
+        front_kernel,
+        out_shape=(
+            jax.ShapeDtypeStruct((NTOK, D), F32),
+            jax.ShapeDtypeStruct((NTOK, D), BF16),
+            jax.ShapeDtypeStruct((col, 16, NTOK), BF16),
+        ),
+        in_specs=[vmem] * 9,
+        out_specs=(vmem, vmem, vmem),
+        scratch_shapes=[
+            pltpu.VMEM((col, PIECE + 16, HEAD), BF16),
+            pltpu.VMEM((col, PIECE + 16, HEAD), BF16),
+            pltpu.VMEM((PIECE, HEAD), F32),
+            pltpu.VMEM((NY, PIECE, HEAD), F32),
+            pltpu.VMEM((PIECE, HEAD), F32),
+            pltpu.VMEM((NX, PIECE, HEAD), F32),
+            pltpu.VMEM((col, PIECE, HEAD), BF16),
+            pltpu.VMEM((col, PIECE, HEAD), BF16),
+            pltpu.VMEM((NTOK, D), F32),
+            sem((col,)), sem((col,)), sem((NY,)), sem((NY,)),
+            sem((NX,)), sem((NX,)), sem((col,)), sem((col,)),
+        ],
+        compiler_params=pltpu.CompilerParams(collective_id=0, has_side_effects=True),
+    )(q, k, v, hid, ngain, wo, mgain, ids, scl)
 
 
 def expert_rows(arrived, w_gate, w_up, w_down):
@@ -51,38 +212,15 @@
 
 
 def body(
-    hidden_in,
-    queries,
-    key_rows,
-    values,
-    norm_gain,
-    out_proj,
-    moe_gain,
-    w_gate,
-    w_up,
-    w_down,
-    expert_ids,
-    route_scale,
+    hidden_in, queries, key_rows, values, norm_gain, out_proj, moe_gain,
+    w_gate, w_up, w_down, expert_ids, route_scale,
 ):
     ntok = queries.shape[0]
     high = lax.Precision.HIGHEST
-    q_loc = queries.astype(jnp.float32).reshape(ntok, HEADS, HEAD)
-    k_loc = key_rows.astype(jnp.float32).reshape(ntok, HEADS, HEAD)
-    v_loc = values.astype(jnp.float32).reshape(ntok, HEADS, HEAD)
-    own_state = jnp.einsum("thd,the->hde", k_loc, v_loc, precision=high)
-    empty = jnp.zeros_like(own_state)
-    earlier = entering(own_state, SEG_CTX, add_states, empty)
-    causal = jnp.arange(ntok)[:, None] >= jnp.arange(ntok)[None, :]
-    scores = jnp.einsum("thd,shd->hts", q_loc, k_loc, precision=high)
-    scores = jnp.where(causal[None, :, :], scores, jnp.zeros((), jnp.float32))
-    inside = jnp.einsum("hts,she->the", scores, v_loc, precision=high)
-    carried = jnp.einsum("thd,hde->the", q_loc, earlier, precision=high)
-    attended = (carried + inside).reshape(ntok, D)
-    normed = rms_scale(attended, norm_gain).astype(jnp.bfloat16)
-    mixed = hidden_in.astype(jnp.float32) + jnp.dot(
-        normed, out_proj, preferred_element_type=jnp.float32
-    )
-    routed = rms_scale(mixed, moe_gain).astype(jnp.bfloat16)
+    mixed, routed, _ = front(
+        queries, key_rows, values, hidden_in, norm_gain[None, :], out_proj, moe_gain[None, :],
+        expert_ids, route_scale,
+    )
     experts_all = lax.axis_size(CTX) * w_gate.shape[0]
     capacity = min(ntok, 3 * ntok * TOP // (2 * experts_all))
     expert_grid = jnp.arange(experts_all, dtype=jnp.int32)

time: 366 us -> 241 us (0.66)
  waiting for transfers between devices: 206 us -> 73.1 us
  Pallas kernels: 0 us -> 41.2 us
  between operations: 13.4 us -> 0.1 us
  matrix products: 28.1 us -> 18.2 us
  other arithmetic: 15.8 us -> 9 us
  blocking collectives: 84.3 us -> 79.3 us
    all_gather x4 -> x0, waiting for transfers between devices: 133 us -> none  [entering(): pieces = lax.all_gather(so_far, axis)]
    pallas_call x0 -> x1, Pallas kernels: none -> 41.2 us  [front(): pl.pallas_call(front_kernel, out_shape=(jax.ShapeDtypeStruct((NTOK, D), F...]
    dot_general x5 -> x0, matrix products: 10.2 us -> none  [the longest x1 4.8 us: body(): carried = jnp.einsum('thd,hde->the', q_loc, earlier, precision=high)]
    add x3 -> x0, other arithmetic: 7.86 us -> none  [add_states(): return earlier + later]
    all_to_all x1, blocking collectives: 84.3 us -> 79.3 us  [body(): lax.all_to_all(outgoing, CTX, split_axis=0, concat_axis=0, tiled=True)]
  transfers between devices with their start and end apart: 5 -> 1, of which waited for: 5 -> 1; matrix products, arithmetic and copies ran while one was open for 2% -> 0% of each run, Pallas kernels for 0% -> 0%
where the time goes in v1:
time: 241 us
  blocking collectives  79.3 us (33%)
  waiting for transfers between devices  73.1 us (30%)
  Pallas kernels  41.2 us (17%)
  matrix products  18.2 us (8%)
  local copies, waits for them, and re-layouts  13.4 us (6%)
  other arithmetic  9 us (4%)
  starting transfers between devices  6.49 us (3%)
    all_to_all x1, blocking collectives, body(): lax.all_to_all(outgoing, CTX, split_axis=0, concat_axis=0, tiled=True)  79.3 us
    all_to_all x1, waiting for transfers between devices, body(): lax.all_to_all(expert_rows(lax.all_to_all(outgoing, CTX, split_axis=0, co...  73.1 us
    pallas_call x1, Pallas kernels, front(): pl.pallas_call(front_kernel, out_shape=(jax.ShapeDtypeStruct((NTOK, D), F...  41.2 us
    dot_general x1, matrix products, expert_rows(): jnp.dot(inner, w_down[0], preferred_element_type=jnp.float32)  10.9 us
    gather x1, local copies, waits for them, and re-layouts, body(): back_rows[slot_id.reshape(-1)].reshape(ntok, TOP, D).astype(jnp.float32)  8.4 us
    all_to_all x1, starting transfers between devices, body(): lax.all_to_all(expert_rows(lax.all_to_all(outgoing, CTX, split_axis=0, co...  6.49 us
    dot_general x1, matrix products, expert_rows(): gate = jnp.dot(rows, w_gate[0], preferred_element_type=jnp.float32)  5.14 us
  transfers between devices with their start and end apart: 1, of which 1 were waited for; matrix products, arithmetic and copies ran while one was open for 0% of the time, Pallas kernels for 0%

profile of v1, /device:TPU:1, one launch (start us, length us, event | category | flops | bytes accessed | tf_op | source)
XLA Modules:
  0.0 240.8 jit_solution(382123423250464382)
XLA Ops:
  0.0 0.0 copy-start
  0.0 1.5 copy.26.ids
  1.6 0.7 convert_reduce_fusion.1
  2.3 1.4 copy.27.scl
  3.7 0.2 fusion.7
  3.9 0.7 select_reduce_fusion
  4.6 0.7 convert_add_fusion
  5.3 0.1 copy.29
  5.4 3.1 %convert_reduce_fusion = bf16[128,1536]{1,0:T(8,128)(2,1)S(1)} fusion(s32[128,8]{1,0:T(8,128)S(1)} %copy.29), kind=kLoop, calls=%fused_computation.1 | loop fusion | flops 4521984 | bytes 397312 | tf_op jit(solution)/shard_map/reduce_sum | solution.py:234
  8.5 41.2 %shard_map.118 = (f32[128,1024]{1,0:T(8,128)}, bf16[128,1024]{1,0:T(8,128)(2,1)}, bf16[16,16,128]{2,1,0:T(8,128)(2,1)}) custom-call(bf16[128,1024]{1,0:T(8,128)(2,1)} %q.1, bf16[128,1024]{1,0:T(8,128)(2,1)} %k.1, bf16[128,1024]{1,0:T(8,128)(2,1)} %v.1, bf16[128,1024]{1,0:T(8,128)(2,1)} %hid.1, f32[1,1024]{1,0:T(1,128)} %bitcast.30, bf16[1024,1024]{1,0:T(8,128)(2,1)} %wo.1, ...), custom_call_target="tpu_custom_call" | custom-call | tf_op jit(solution)/shard_map/pallas_call | solution.py:178
  49.8 1.9 convolution_convert_fusion
  51.7 0.0 copy-start.4
  51.8 79.3 %all_to_all.10 = bf16[64,24,1024]{2,1,0:T(8,128)(2,1)S(1)} all-to-all(bf16[64,24,1024]{2,1,0:T(8,128)(2,1)S(1)} %bitcast.25), channel_id=1, replica_groups=mesh['seg'=4,'ctx_0'=4,'ctx_1'=8,'ctx_2'=2] {'ctx_0','ctx_1','ctx_2'}, dimensions={0} | all-to-all | bytes 6291456 | tf_op jit(solution)/shard_map/all_to_all | solution.py:241
  131.1 0.0 copy-start.1
  131.1 1.7 copy-done.1
  132.8 0.0 copy-done.4
  132.8 5.1 %fusion.4 = f32[1536,896]{1,0:T(8,128)} fusion(bf16[1536,1024]{1,0:T(8,128)(2,1)S(1)} %bitcast.27, bf16[1,1024,896]{2,1,0:T(8,128)(2,1)S(1)} %copy-done.4), kind=kOutput, calls=%fused_computation.10 | convolution fusion | flops 2818572288 | bytes 10485760 | tf_op jit(solution)/shard_map/dot_general | solution.py:207
  137.9 0.0 copy-done
  137.9 10.9 %convolution_convert_fusion.1 = bf16[1536,1024]{1,0:T(8,128)(2,1)} fusion(f32[1536,896]{1,0:T(8,128)} %fusion.4, bf16[1536,1024]{1,0:T(8,128)(2,1)} %bitcast.28, bf16[1,896,1024]{2,1,0:T(8,128)(2,1)S(1)} %copy-done, bf16[1,1024,896]{2,1,0:T(8,128)(2,1)} %param.20), kind=kOutput, calls=%fused_computation.7 | convolution fusion | flops 5646974976 | bytes 15466496 | tf_op jit(solution)/shard_map/dot_general | solution.py:210
  148.8 0.0 copy-start.3
  148.8 6.5 %all-to-all-start.1 = ((bf16[64,24,1024]{2,1,0:T(8,128)(2,1)}), bf16[64,24,1024]{2,1,0:T(8,128)(2,1)}, u32[]{:S(2)}, u32[]{:S(2)}) async-start(bf16[64,24,1024]{2,1,0:T(8,128)(2,1)} %bitcast.26), calls=%async_computation.1 | async-start | bytes 6291456 | tf_op jit(solution)/shard_map/all_to_all | solution.py:239
  155.3 0.1 reshape.55
  155.4 0.0 copy-done.3
  155.4 0.1 copy.28
  155.6 73.1 %all-to-all-done.1 = bf16[64,24,1024]{2,1,0:T(8,128)(2,1)} async-done(((bf16[64,24,1024]{2,1,0:T(8,128)(2,1)}), bf16[64,24,1024]{2,1,0:T(8,128)(2,1)}, u32[]{:S(2)}, u32[]{:S(2)}) %all-to-all-start.1) | async-done | bytes 3145760 | tf_op jit(solution)/shard_map/all_to_all | solution.py:239
  228.7 0.0 copy-start.2
  228.7 8.4 %gather_fusion = bf16[1024,1024]{1,0:T(8,128)(2,1)} fusion(bf16[1536,1024]{1,0:T(8,128)(2,1)} %bitcast.8, s32[1024]{0:T(1024)S(1)} %broadcast_clamp_fusion), kind=kCustom, calls=%fused_computation | custom fusion | bytes 4198400 | tf_op jit(solution)/shard_map/gather | solution.py:252
  237.1 2.9 %fusion = f32[128,1024]{1,0:T(8,128)S(1)} fusion(bf16[1024,1024]{1,0:T(8,128)(2,1)} %gather_fusion, f32[128,8]{1,0:T(8,128)S(1)} %copy.28), kind=kLoop, calls=%fused_computation.5 | loop fusion | flops 3014656 | bytes 2625536 | tf_op jit(solution)/shard_map/reduce_sum | solution.py:255
  240.1 0.0 copy-done.2
  240.1 0.8 add_convert_fusion
  (4 shorter events, 0.0 us)
Async XLA Ops:
  0.0 137.9 %copy-start = (bf16[1,896,1024]{2,1,0:T(8,128)(2,1)S(1)}, bf16[1,896,1024]{2,1,0:T(8,128)(2,1)}, u32[]{:S(2)}) copy-start(bf16[1,896,1024]{2,1,0:T(8,128)(2,1)} %param.21) | copy-start | bytes 5505028
  51.7 81.0 %copy-start.4 = (bf16[1,1024,896]{2,1,0:T(8,128)(2,1)S(1)}, bf16[1,1024,896]{2,1,0:T(8,128)(2,1)}, u32[]{:S(2)}) copy-start(bf16[1,1024,896]{2,1,0:T(8,128)(2,1)} %param.19) | copy-start | bytes 5505028
  131.1 1.7 copy-start.1
  148.8 6.6 %copy-start.3 = (s32[128,8]{0,1:T(8,128)S(1)}, s32[128,8]{0,1:T(8,128)}, u32[]{:S(2)}) copy-start(s32[128,8]{0,1:T(8,128)} %param.23) | copy-start | bytes 12292
  148.8 79.9 %all-to-all-start.1 = ((bf16[64,24,1024]{2,1,0:T(8,128)(2,1)}), bf16[64,24,1024]{2,1,0:T(8,128)(2,1)}, u32[]{:S(2)}, u32[]{:S(2)}) async-start(bf16[64,24,1024]{2,1,0:T(8,128)(2,1)} %bitcast.26), calls=%async_computation.1 | async-start | bytes 6291456 | tf_op jit(solution)/shard_map/all_to_all | solution.py:239
  228.7 11.3 %copy-start.2 = (f32[128,1024]{1,0:T(8,128)S(1)}, f32[128,1024]{1,0:T(8,128)}, u32[]{:S(2)}) copy-start(f32[128,1024]{1,0:T(8,128)} %get-tuple-element.7) | copy-start | bytes 1572868

commit v2 on v1

--- a/solution.py
+++ b/solution.py
@@ -93,7 +93,7 @@
         chosen = jnp.where(hit, 1.0, chosen)
         scale = jnp.where(hit, sct[j : j + 1, :], scale)
     earlier = (iota((NTOK, NTOK), 0) < iota((NTOK, NTOK), 1)).astype(BF16)
-    pos = jnp.where(chosen > 0.5, dot(chosen.astype(BF16), earlier), -1.0)
+    pos = jnp.where(chosen > 0.5, dot(chosen.astype(BF16), earlier), -64.0)
     weight = scale / jnp.sum(sct, axis=0, keepdims=True)
     whi = weight.astype(BF16).astype(F32)
     table = jnp.where(kind == 0, pos, jnp.where(kind == 1, whi, jnp.where(kind == 2, weight - whi, 0.0)))
@@ -201,59 +201,267 @@
     )(q, k, v, hid, ngain, wo, mgain, ids, scl)
 
 
-def expert_rows(arrived, w_gate, w_up, w_down):
-    sources, slots = (arrived.shape[0], arrived.shape[1])
-    rows = arrived.reshape(sources * slots, D)
-    gate = jnp.dot(rows, w_gate[0], preferred_element_type=jnp.float32)
-    upper = jnp.dot(rows, w_up[0], preferred_element_type=jnp.float32)
-    inner = (jax.nn.silu(gate) * upper).astype(jnp.bfloat16)
-    result = jnp.dot(inner, w_down[0], preferred_element_type=jnp.float32).astype(jnp.bfloat16)
-    return result.reshape(sources, slots, D)
+NK = NZ
+SLOTS = 48
+GROUP = NY * SLOTS
+FF = 896
+
+
+def back_kernel(
+    routed, meta, mixed, wg_h, wu_h, wd_h,
+    out,
+    blk, pick, pick_lo, sel, rows, inner, outs, ret, pown, pb, pin, part, racc, wg, wu, wd,
+    sw, sag, rag, sm, rm, sy, ry, sr, rr, sp, rp, sc, rc,
+):
+    x, y, z, c = place()
+    right = (x, y, lax.rem(z + 1, NZ), c)
+    left = (x, y, lax.rem(z + NZ - 1, NZ), c)
+    mate = (x, y, z, 1 - c)
+    ahead = [(x, lax.rem(y + o, NY), z, c) for o in range(NY)]
+    behind = [(x, lax.rem(y + NY - o, NY), z, c) for o in range(NY)]
+    loads = [
+        pltpu.make_async_copy(a.at[0], b, sw.at[i])
+        for i, (a, b) in enumerate(((wg_h, wg), (wu_h, wu), (wd_h, wd)))
+    ]
+    for cp in loads:
+        cp.start()
+    barrier([right, left, mate] + ahead[1:])
+
+    def gather_copy(k, dev):
+        return remote(blk.at[k, 0], blk.at[k + 2, 0], sag.at[k], rag.at[k + 2], dev)
+
+    def half_copy(k, half, sem, dev):
+        part_of = pl.ds(half * 64, 64)
+        return remote(blk.at[k, 0, part_of], blk.at[7, 0, part_of], sag.at[k], rag.at[sem], dev)
+
+    def mate_copy(k):
+        return remote(blk.at[k, 0], blk.at[k, 1], sm.at[k], rm.at[k], mate)
+
+    def arrival(k):
+        return remote(routed, blk.at[k, 0], sag.at[0], rag.at[k], right)
+
+    def own_copy(k, dev):
+        return remote(routed, blk.at[k, 0], sag.at[6 + k], rag.at[k], dev)
+
+    def out_copy(k, o):
+        span = pl.ds(o * SLOTS, SLOTS)
+        return remote(sel.at[k, span], rows.at[k, span], sy.at[k, o], ry.at[k, o], ahead[o])
+
+    def back_copy(k, o):
+        span = pl.ds(o * SLOTS, SLOTS)
+        return remote(outs.at[k, span], ret.at[k, span], sr.at[k, o], rr.at[k, o], behind[o])
+
+    def source(k):
+        return lax.rem(z + NZ + ((k + 1) // 2) * (1 - 2 * lax.rem(k, 2)), NZ) * NC
+
+    slot = iota((SLOTS, NTOK), 0).astype(F32)
+
+    own_copy(1, right).start()
+    own_copy(2, left).start()
+    own_mate = remote(routed, blk.at[0, 1], sm.at[0], rm.at[0], mate)
+    own_mate.start()
+    blk[0, 0] = routed[...]
+
+    def pass_on(k):
+        @pl.when(k < 7)
+        def _():
+            arrival(k).wait_recv()
+
+        @pl.when(k == 7)
+        def _():
+            half_copy(5, 0, 7, right).wait_recv()
+            half_copy(6, 1, 8, left).wait_recv()
+
+        @pl.when((k < 5) & (lax.rem(k, 2) == 1))
+        def _():
+            gather_copy(k, right).start()
+
+        @pl.when((k < 5) & (lax.rem(k, 2) == 0))
+        def _():
+            gather_copy(k, left).start()
+
+        @pl.when(k == 5)
+        def _():
+            half_copy(5, 0, 7, right).start()
+
+        @pl.when(k == 6)
+        def _():
+            half_copy(6, 1, 8, left).start()
+
+        mate_copy(k).start()
+
+    def select(k):
+        mate_copy(k).wait_recv()
+        src = source(k)
+        mine, other = meta[src + c].astype(F32), meta[src + 1 - c].astype(F32)
+        mine_at, other_at = slot - (24 * c).astype(F32), slot - (24 * (1 - c)).astype(F32)
+        for o in range(NY):
+            span = slice(o * SLOTS, (o + 1) * SLOTS)
+            pick[span, :NTOK] = (mine[o : o + 1, :] == mine_at).astype(F32).astype(BF16)
+            pick[span, NTOK:] = (other[o : o + 1, :] == other_at).astype(F32).astype(BF16)
+        for n in range(0, D, 256):
+            cols = slice(n, n + 256)
+            got = dot(pick[...], blk[k, :, :, cols].reshape(2 * NTOK, 256)).astype(BF16)
+            sel[k, SLOTS:, cols] = got[SLOTS:]
+            rows[k, :SLOTS, cols] = got[:SLOTS]
+        for o in range(1, NY):
+            out_copy(k, o).start()
+
+    def expert(k):
+        for o in range(1, NY):
+            out_copy(k, o).wait_recv()
+        got = rows[k]
+        for n in range(0, FF, 256):
+            cols = slice(n, min(FF, n + 256))
+            gate, upper = dot(got, wg[:, cols]), dot(got, wu[:, cols])
+            inner[:, cols] = (gate / (1.0 + jnp.exp(-gate)) * upper).astype(BF16)
+        for n in range(0, D, 256):
+            cols = slice(n, n + 256)
+            res = dot(inner[...], wd[:, cols]).astype(BF16)
+            outs[k, SLOTS:, cols] = res[SLOTS:]
+            ret[k, :SLOTS, cols] = res[:SLOTS]
+
+    def step(it, carry):
+        @pl.when(it < NK)
+        def _():
+            select(it)
+
+        @pl.when(it == 0)
+        def _():
+            pass_on(1)
+            pass_on(2)
+            for cp in loads:
+                cp.wait()
+
+        @pl.when(it > 0)
+        def _():
+            expert(it - 1)
+
+        @pl.when((it > 0) & (it < NK - 2))
+        def _():
+            pass_on(it + 2)
+
+        return carry
+
+    lax.fori_loop(0, NK + 1, step, 0)
+    for k in range(NK - 1, -1, -1):
+        for o in range(1, NY):
+            back_copy(k, o).start()
+
+    def weigh(k):
+        for o in range(1, NY):
+            back_copy(k, o).wait_recv()
+        src = source(k)
+        mine, other = meta[src + c].astype(F32), meta[src + 1 - c].astype(F32)
+        mine_at, other_at = slot - (24 * c).astype(F32), slot - (24 * (1 - c)).astype(F32)
+        for ref, kind in ((pick, NY), (pick_lo, 2 * NY)):
+            for o in range(NY):
+                span = slice(o * SLOTS, (o + 1) * SLOTS)
+                at = kind + o
+                ref[span, :NTOK] = jnp.where(mine[o : o + 1, :] == mine_at, mine[at : at + 1, :], 0.0).astype(BF16)
+                ref[span, NTOK:] = jnp.where(other[o : o + 1, :] == other_at, other[at : at + 1, :], 0.0).astype(BF16)
+        for n in range(0, D, 256):
+            cols = slice(n, n + 256)
+            got = ret[k, :, cols]
+            summed = dot(pick[...], got, ((0,), (0,))) + dot(pick_lo[...], got, ((0,), (0,)))
+            pown[:, cols] = summed[:NTOK]
+            pb[k, :, cols] = summed[NTOK:].astype(BF16)
+        send = remote(pb.at[k], pin.at[k], sp.at[k], rp.at[k], mate)
+        send.start()
+        return send
+
+    def ring_half(half):
+        span = pl.ds(half * 64, 64)
+        return remote(
+            part.at[7, span], racc.at[5 + half, span], sc.at[7 + half], rc.at[5 + half], right if half else left
+        )
+
+    def ring_copy(k):
+        to = {1: 0, 2: 7}.get(k, k - 2)
+        return remote(part.at[k], racc.at[to], sc.at[k], rc.at[to], left if k % 2 else right)
+
+    sent, mates = [], []
+    for k in range(NK - 1, -1, -1):
+        cp = weigh(k)
+        mates.append(cp)
+        cp.wait_recv()
+        if k == 7:
+            part[7] = (pown[...] + pin[7].astype(F32)).astype(BF16)
+        elif k == 5 or k == 6:
+            half = k - 5
+            ring_half(half).wait_recv()
+            add, keep = slice(half * 64, half * 64 + 64), slice(64 - half * 64, 128 - half * 64)
+            part[k, keep] = (pown[keep] + pin[k, keep].astype(F32)).astype(BF16)
+            part[k, add] = (pown[add] + pin[k, add].astype(F32) + racc[k, add].astype(F32)).astype(BF16)
+        elif k:
+            ring_copy(k + 2).wait_recv()
+            part[k] = (pown[...] + pin[k].astype(F32) + racc[k].astype(F32)).astype(BF16)
+        else:
+            ring_copy(1).wait_recv()
+            ring_copy(2).wait_recv()
+            both = racc[0].astype(F32) + racc[7].astype(F32)
+            out[...] = (mixed[...] + (pown[...] + pin[0].astype(F32) + both)).astype(BF16)
+        if k:
+            for cp in [ring_half(0), ring_half(1)] if k == 7 else [ring_copy(k)]:
+                cp.start()
+                sent.append(cp)
+
+    own_copy(1, right).wait_send()
+    own_copy(2, left).wait_send()
+    for k in range(1, 5):
+        gather_copy(k, right).wait_send()
+    half_copy(5, 0, 7, right).wait_send()
+    half_copy(6, 1, 8, left).wait_send()
+    for k in range(NK):
+        mate_copy(k).wait_send()
+        for o in range(1, NY):
+            out_copy(k, o).wait_send()
+            back_copy(k, o).wait_send()
+    for cp in sent + mates:
+        cp.wait_send()
+
+
+def back(routed, meta, mixed, w_gate, w_up, w_down):
+    sem = pltpu.SemaphoreType.DMA
+    vmem, away = pl.BlockSpec(memory_space=pltpu.VMEM), pl.BlockSpec(memory_space=pl.ANY)
+    return pl.pallas_call(
+        back_kernel,
+        out_shape=jax.ShapeDtypeStruct((NTOK, D), BF16),
+        in_specs=[vmem, vmem, vmem, away, away, away],
+        out_specs=vmem,
+        scratch_shapes=[
+            pltpu.VMEM((NK, 2, NTOK, D), BF16),
+            pltpu.VMEM((GROUP, 2 * NTOK), BF16),
+            pltpu.VMEM((GROUP, 2 * NTOK), BF16),
+            pltpu.VMEM((NK, GROUP, D), BF16),
+            pltpu.VMEM((NK, GROUP, D), BF16),
+            pltpu.VMEM((GROUP, FF), BF16),
+            pltpu.VMEM((NK, GROUP, D), BF16),
+            pltpu.VMEM((NK, GROUP, D), BF16),
+            pltpu.VMEM((NTOK, D), F32),
+            pltpu.VMEM((NK, NTOK, D), BF16),
+            pltpu.VMEM((NK, NTOK, D), BF16),
+            pltpu.VMEM((NK, NTOK, D), BF16),
+            pltpu.VMEM((NK, NTOK, D), BF16),
+            pltpu.VMEM((D, FF), BF16),
+            pltpu.VMEM((D, FF), BF16),
+            pltpu.VMEM((FF, D), BF16),
+            sem((3,)), sem((9,)), sem((9,)), sem((NK,)), sem((NK,)), sem((NK, NY)), sem((NK, NY)),
+            sem((NK, NY)), sem((NK, NY)), sem((NK,)), sem((NK,)), sem((9,)), sem((9,)),
+        ],
+        compiler_params=pltpu.CompilerParams(collective_id=1, has_side_effects=True),
+    )(routed, meta, mixed, w_gate, w_up, w_down)
 
 
 def body(
     hidden_in, queries, key_rows, values, norm_gain, out_proj, moe_gain,
     w_gate, w_up, w_down, expert_ids, route_scale,
 ):
-    ntok = queries.shape[0]
-    high = lax.Precision.HIGHEST
-    mixed, routed, _ = front(
+    mixed, routed, meta = front(
         queries, key_rows, values, hidden_in, norm_gain[None, :], out_proj, moe_gain[None, :],
         expert_ids, route_scale,
     )
-    experts_all = lax.axis_size(CTX) * w_gate.shape[0]
-    capacity = min(ntok, 3 * ntok * TOP // (2 * experts_all))
-    expert_grid = jnp.arange(experts_all, dtype=jnp.int32)
-    chosen = (expert_ids[:, :, None] == expert_grid[None, None, :]).astype(jnp.float32)
-    per_token = jnp.sum(chosen, axis=1)
-    lower = (jnp.arange(ntok)[:, None] > jnp.arange(ntok)[None, :]).astype(jnp.float32)
-    before_tok = jnp.dot(lower, per_token, precision=high)
-    position = jnp.sum(chosen * before_tok[:, None, :], axis=2).astype(jnp.int32)
-    slot_id = expert_ids * capacity + position
-    slot_grid = jnp.arange(experts_all * capacity, dtype=jnp.int32)
-    placing = jnp.sum(
-        (slot_id[:, :, None] == slot_grid[None, None, :]).astype(jnp.float32), axis=1
-    ).astype(jnp.bfloat16)
-    outgoing = jnp.einsum("ts,td->sd", placing, routed, preferred_element_type=jnp.float32)
-    outgoing = outgoing.astype(jnp.bfloat16).reshape(experts_all, capacity, D)
-    came_back = lax.all_to_all(
-        expert_rows(
-            lax.all_to_all(outgoing, CTX, split_axis=0, concat_axis=0, tiled=True),
-            w_gate,
-            w_up,
-            w_down,
-        ),
-        CTX,
-        split_axis=0,
-        concat_axis=0,
-        tiled=True,
-    )
-    back_rows = came_back.reshape(experts_all * capacity, D)
-    picked = back_rows[slot_id.reshape(-1)].reshape(ntok, TOP, D).astype(jnp.float32)
-    scales = route_scale.astype(jnp.float32)
-    weight = scales / jnp.sum(scales, axis=1, keepdims=True)
-    combined = jnp.sum(weight[:, :, None] * picked, axis=1)
-    return (mixed + combined).astype(jnp.bfloat16)
+    return back(routed, meta, mixed, w_gate, w_up, w_down)
 
 
 def solution(mesh):

time: 241 us -> 135 us (0.56)
  Pallas kernels: 41.2 us -> 131 us
  blocking collectives: 79.3 us -> 0 us
  waiting for transfers between devices: 73.1 us -> 0 us
  matrix products: 18.2 us -> 0 us
  other arithmetic: 9 us -> 0 us
  local copies, waits for them, and re-layouts: 13.4 us -> 4.5 us
  starting transfers between devices: 6.49 us -> 0 us
    pallas_call x0 -> x1, Pallas kernels: none -> 89.6 us  [back(): pl.pallas_call(back_kernel, out_shape=jax.ShapeDtypeStruct((NTOK, D), BF1...]
    all_to_all x1 -> x0, blocking collectives: 79.3 us -> none  [body(): lax.all_to_all(outgoing, CTX, split_axis=0, concat_axis=0, tiled=True)]
    all_to_all x1 -> x0, waiting for transfers between devices: 73.1 us -> none  [body(): lax.all_to_all(expert_rows(lax.all_to_all(outgoing, CTX, split_axis=0, co...]
    dot_general x4 -> x0, matrix products: 18.2 us -> none  [the longest x1 10.9 us: expert_rows(): jnp.dot(inner, w_down[0], preferred_element_type=jnp.float32)]
    gather x1 -> x0, local copies, waits for them, and re-layouts: 8.4 us -> none  [body(): back_rows[slot_id.reshape(-1)].reshape(ntok, TOP, D).astype(jnp.float32)]
    reduce_sum x5 -> x0, other arithmetic: 7.51 us -> none  [the longest x1 3.12 us: body(): jnp.sum((slot_id[:, :, None] == slot_grid[None, None, :]).astype(jnp.floa...]
    all_to_all x1 -> x0, starting transfers between devices: 6.49 us -> none  [body(): lax.all_to_all(expert_rows(lax.all_to_all(outgoing, CTX, split_axis=0, co...]
  transfers between devices with their start and end apart: 1 -> 0, of which waited for: 1 -> 0; matrix products, arithmetic and copies ran while one was open for 0% -> 0% of each run, Pallas kernels for 0% -> 0%
where the time goes in v2:
time: 135 us
  Pallas kernels  131 us (97%)
  local copies, waits for them, and re-layouts  4.5 us (3%)
    pallas_call x1, Pallas kernels, back(): pl.pallas_call(back_kernel, out_shape=jax.ShapeDtypeStruct((NTOK, D), BF1...  89.6 us
    pallas_call x1, Pallas kernels, front(): pl.pallas_call(front_kernel, out_shape=(jax.ShapeDtypeStruct((NTOK, D), F...  41.1 us
    unnamed x3, local copies, waits for them, and re-layouts  4.5 us

profile of v2, /device:TPU:1, one launch (start us, length us, event | category | flops | bytes accessed | tf_op | source)
XLA Modules:
  0.0 135.2 jit_solution(4259653214009460161)
XLA Ops:
  0.0 1.4 %copy.13.ids = s32[128,8]{1,0:T(8,128)} copy(s32[128,8]{0,1:T(8,128)} %param.22) | data formatting | bytes 8192 | tf_op args[10]
  1.4 1.4 %copy.14.scl = s32[128,8]{1,0:T(8,128)} copy(s32[128,8]{0,1:T(8,128)} %param.23) | data formatting | bytes 8192 | tf_op args[11]
  2.8 41.1 %shard_map.118 = (f32[128,1024]{1,0:T(8,128)}, bf16[128,1024]{1,0:T(8,128)(2,1)}, bf16[16,16,128]{2,1,0:T(8,128)(2,1)}) custom-call(bf16[128,1024]{1,0:T(8,128)(2,1)} %q.1, bf16[128,1024]{1,0:T(8,128)(2,1)} %k.1, bf16[128,1024]{1,0:T(8,128)(2,1)} %v.1, bf16[128,1024]{1,0:T(8,128)(2,1)} %hid.1, f32[1,1024]{1,0:T(1,128)} %bitcast.2, bf16[1024,1024]{1,0:T(8,128)(2,1)} %wo.1, ...), custom_call_target="tpu_custom_call" | custom-call | tf_op jit(solution)/shard_map/pallas_call | solution.py:178
  43.9 89.6 %shard_map.119 = bf16[128,1024]{1,0:T(8,128)(2,1)} custom-call(bf16[128,1024]{1,0:T(8,128)(2,1)} %get-tuple-element.8.routed, bf16[16,16,128]{2,1,0:T(8,128)(2,1)} %get-tuple-element.9.meta, f32[128,1024]{1,0:T(8,128)} %get-tuple-element.10.mixed, bf16[1,1024,896]{2,1,0:T(8,128)(2,1)} %wg_h.1, bf16[1,1024,896]{2,1,0:T(8,128)(2,1)} %wu_h.1, ...), custom_call_target="tpu_custom_call" | custom-call | tf_op jit(solution)/shard_map/pallas_call | solution.py:427
  133.6 1.7 %copy.16 = bf16[128,1024]{1,0:T(8,128)(2,1)} copy(bf16[128,1024]{1,0:T(8,128)(2,1)} %shard_map.119) | data formatting | bytes 524288
